TPU v7x, 256 devices: a whole 4x4x8 slice. The times are simulated.
256 devices in a mesh: seq: 128 (over z, y_hi, x, core), head: 2 (over y_lo).
Axes of the slice: x: 4, y: 4 (y_hi: 2, y_lo: 2; y = y_hi * 2 + y_lo), z: 8, core: 2. Of those that a mesh axis runs over, the one named last changes fastest.
Arguments:
- queries: bfloat16 [16384, 2048], P(('seq', 'head')), may hold values from -8 to 8
- key_rows: bfloat16 [16384, 2048], P(('seq', 'head')), may hold values from -8 to 8
- values: bfloat16 [16384, 2048], P(('seq', 'head')), may hold values from -6 to 6
- out_grad: bfloat16 [16384, 2048], P(('seq', 'head')), may hold values from -6 to 6
Outputs:
- attended: bfloat16 [16384, 2048], P(('seq', 'head'))
- query_grad: bfloat16 [16384, 2048], P(('seq', 'head'))
- key_grad: bfloat16 [16384, 2048], P(('seq', 'head'))
- value_grad: bfloat16 [16384, 2048], P(('seq', 'head'))
All inputs are finite; a program needn't handle non-finite values.
Results may differ from a plain program's by a relative error of at most 0.028.
Values may be sent and summed in bfloat16 or wider, within the bound.
A program may use at most 64 MiB of HBM per device.

v0:
```python
import math
import jax
import jax.numpy as jnp
from jax import lax
from jax.sharding import PartitionSpec as P

HEAD_DIM = 128
ROOT_HALF = 0.7071067811865476


def swapped(block, axis, distance):
    count = lax.axis_size(axis)
    route = []
    for low in range(count):
        high = low | 1 << distance
        if high != low and high < count:
            route += [(low, high), (high, low)]
    return lax.ppermute(block, axis, route)


def pool_rows(blocks):
    widened = blocks.astype(jnp.float32)
    paired = widened.reshape((widened.shape[0] // 2, 2) + widened.shape[1:])
    return ((paired[:, 0] + paired[:, 1]) * ROOT_HALF).astype(jnp.bfloat16)


def unpool_rows(blocks):
    return jnp.repeat(blocks, 2, axis=0) * ROOT_HALF


def local(queries, key_rows, values, out_grad):
    query_in, key_in, value_in, grad_in = (
        lax.all_to_all(queries, "head", split_axis=1, concat_axis=0, tiled=True),
        lax.all_to_all(key_rows, "head", split_axis=1, concat_axis=0, tiled=True),
        lax.all_to_all(values, "head", split_axis=1, concat_axis=0, tiled=True),
        lax.all_to_all(out_grad, "head", split_axis=1, concat_axis=0, tiled=True),
    )
    token_rows = query_in.shape[0]
    head_count = query_in.shape[1] // HEAD_DIM
    local_shape = (token_rows, head_count, HEAD_DIM)
    query_loc = query_in.reshape(local_shape)
    key_loc = key_in.reshape(local_shape)
    value_loc = value_in.reshape(local_shape)
    grad_loc = grad_in.reshape(local_shape)
    level_count = lax.axis_size("seq").bit_length() - 1
    seq_index = lax.axis_index("seq")
    half_rows = token_rows // 2
    scale_factor = 1.0 / math.sqrt(HEAD_DIM)
    top_bit = seq_index >> level_count - 1 & 1
    sibling_start = (1 - top_bit) * half_rows
    query_pool = [query_loc]
    key_pool = [key_loc]
    value_pool = [value_loc]
    for level_no in range(1, level_count + 1):
        query_pool.append(pool_rows(query_pool[-1]))
        key_pool.append(pool_rows(key_pool[-1]))
        value_pool.append(pool_rows(value_pool[-1]))
    own_keys = key_pool[1]
    own_values = value_pool[1]
    records = []
    for level_no in range(1, level_count + 1):
        if level_no < level_count:
            sib_keys, sib_values = swapped((own_keys, own_values), "seq", level_no - 1)
        else:
            whole_keys, whole_values = (
                lax.all_gather(key_pool[level_count], "seq", axis=0, tiled=True),
                lax.all_gather(value_pool[level_count], "seq", axis=0, tiled=True),
            )
            sib_keys = lax.dynamic_slice_in_dim(whole_keys, sibling_start, half_rows, 0)
            sib_values = lax.dynamic_slice_in_dim(whole_values, sibling_start, half_rows, 0)
        coarse_scores = (
            jnp.einsum(
                "ghd,chd->ghc", query_pool[level_no], sib_keys, preferred_element_type=jnp.float32
            )
            * scale_factor
        )
        coarse_top = jnp.max(coarse_scores, axis=-1)
        coarse_expo = jnp.exp(coarse_scores - coarse_top[..., None])
        coarse_total = jnp.sum(coarse_expo, axis=-1)
        expo_half = coarse_expo.astype(jnp.bfloat16)
        coarse_numer = jnp.einsum(
            "ghc,chd->ghd", expo_half, sib_values, preferred_element_type=jnp.float32
        )
        records.append(
            (sib_keys, sib_values, coarse_expo, expo_half, coarse_top, coarse_total, coarse_numer)
        )
        if level_no < level_count - 1:
            own_bit = seq_index >> level_no - 1 & 1
            lower_keys = jnp.where(own_bit == 0, own_keys, sib_keys)
            upper_keys = jnp.where(own_bit == 0, sib_keys, own_keys)
            lower_values = jnp.where(own_bit == 0, own_values, sib_values)
            upper_values = jnp.where(own_bit == 0, sib_values, own_values)
            own_keys = pool_rows(jnp.concatenate([lower_keys, upper_keys], axis=0))
            own_values = pool_rows(jnp.concatenate([lower_values, upper_values], axis=0))
    local_scores = (
        jnp.einsum("thd,uhd->thu", query_loc, key_loc, preferred_element_type=jnp.float32)
        * scale_factor
    )
    row_top = jnp.max(local_scores, axis=-1)
    for level_no in range(1, level_count + 1):
        row_top = jnp.maximum(row_top, jnp.repeat(records[level_no - 1][4], 2**level_no, axis=0))
    local_expo = jnp.exp(local_scores - row_top[..., None])
    row_total = jnp.sum(local_expo, axis=-1)
    numer_all = jnp.einsum(
        "thu,uhd->thd",
        local_expo.astype(jnp.bfloat16),
        value_loc,
        preferred_element_type=jnp.float32,
    )
    factors = []
    for level_no in range(1, level_count + 1):
        group_rows = 2**level_no
        record = records[level_no - 1]
        factor = jnp.exp(jnp.repeat(record[4], group_rows, axis=0) - row_top)
        row_total = row_total + factor * jnp.repeat(record[5], group_rows, axis=0)
        numer_all = numer_all + factor[..., None] * jnp.repeat(record[6], group_rows, axis=0)
        factors.append(factor)
    outcome = numer_all / row_total[..., None]
    attended = outcome.astype(jnp.bfloat16).reshape(token_rows, -1)
    grad_wide = grad_loc.astype(jnp.float32)
    row_dots = jnp.sum(grad_wide * outcome, axis=-1)
    local_probs = local_expo / row_total[..., None]
    local_dprob = jnp.einsum(
        "thd,uhd->thu", grad_loc, value_loc, preferred_element_type=jnp.float32
    )
    dlocal = (local_probs * (local_dprob - row_dots[..., None])).astype(jnp.bfloat16)
    query_acc = (
        jnp.einsum("thu,uhd->thd", dlocal, key_loc, preferred_element_type=jnp.float32)
        * scale_factor
    )
    key_acc = (
        jnp.einsum("thu,thd->uhd", dlocal, query_loc, preferred_element_type=jnp.float32)
        * scale_factor
    )
    value_acc = jnp.einsum(
        "thu,thd->uhd",
        local_probs.astype(jnp.bfloat16),
        grad_loc,
        preferred_element_type=jnp.float32,
    )
    level_grads = []
    for level_no in range(1, level_count + 1):
        sib_keys, sib_values, coarse_expo, expo_half = records[level_no - 1][:4]
        group_rows = 2**level_no
        coarse_rows = token_rows // group_rows
        weight = factors[level_no - 1] / row_total
        adjoint = (
            (weight[..., None] * grad_wide)
            .reshape(coarse_rows, group_rows, head_count, HEAD_DIM)
            .sum(axis=1)
            .astype(jnp.bfloat16)
        )
        offset = (weight * row_dots).reshape(coarse_rows, group_rows, head_count).sum(axis=1)
        inner_dot = (
            jnp.einsum("ghd,chd->ghc", adjoint, sib_values, preferred_element_type=jnp.float32)
            - offset[..., None]
        )
        dcoarse = (coarse_expo * inner_dot).astype(jnp.bfloat16)
        dquery_level = (
            jnp.einsum("ghc,chd->ghd", dcoarse, sib_keys, preferred_element_type=jnp.float32)
            * scale_factor
        )
        dkey_sib = (
            jnp.einsum(
                "ghc,ghd->chd", dcoarse, query_pool[level_no], preferred_element_type=jnp.float32
            )
            * scale_factor
        )
        dvalue_sib = jnp.einsum(
            "ghc,ghd->chd", expo_half, adjoint, preferred_element_type=jnp.float32
        )
        level_grads.append((dquery_level, dkey_sib, dvalue_sib))
    query_carry = jnp.zeros((token_rows >> level_count, head_count, HEAD_DIM), jnp.float32)
    for level_no in range(level_count, 0, -1):
        query_carry = unpool_rows(query_carry + level_grads[level_no - 1][0])
    query_total = query_acc + query_carry
    tail_keys = None
    tail_values = None
    own_grad_keys = None
    own_grad_values = None
    spread_keys = jnp.zeros(local_shape, jnp.float32)
    spread_values = jnp.zeros(local_shape, jnp.float32)
    spread_keys = lax.dynamic_update_slice_in_dim(spread_keys, level_grads[-1][1], sibling_start, 0)
    spread_values = lax.dynamic_update_slice_in_dim(
        spread_values, level_grads[-1][2], sibling_start, 0
    )
    tail_keys, tail_values = (
        lax.psum_scatter(spread_keys, "seq", scatter_dimension=0, tiled=True),
        lax.psum_scatter(spread_values, "seq", scatter_dimension=0, tiled=True),
    )
    for level_no in range(level_count - 1, 0, -1):
        send_keys = level_grads[level_no - 1][1]
        send_values = level_grads[level_no - 1][2]
        keep_keys = None
        keep_values = None
        if own_grad_keys is not None:
            own_bit = seq_index >> level_no - 1 & 1
            wide_keys = unpool_rows(own_grad_keys)
            wide_values = unpool_rows(own_grad_values)
            keep_keys = jnp.where(own_bit == 0, wide_keys[:half_rows], wide_keys[half_rows:])
            keep_values = jnp.where(own_bit == 0, wide_values[:half_rows], wide_values[half_rows:])
            send_keys = send_keys + jnp.where(
                own_bit == 0, wide_keys[half_rows:], wide_keys[:half_rows]
            )
            send_values = send_values + jnp.where(
                own_bit == 0, wide_values[half_rows:], wide_values[:half_rows]
            )
        recv_keys, recv_values = (
            swapped(send_keys.astype(jnp.bfloat16), "seq", level_no - 1).astype(send_keys.dtype),
            swapped(send_values.astype(jnp.bfloat16), "seq", level_no - 1).astype(
                send_values.dtype
            ),
        )
        if keep_keys is None:
            own_grad_keys = recv_keys
            own_grad_values = recv_values
        else:
            own_grad_keys = keep_keys + recv_keys
            own_grad_values = keep_values + recv_values
    for level_no in range(level_count, 1, -1):
        tail_keys = unpool_rows(tail_keys)
        tail_values = unpool_rows(tail_values)
    base_keys = tail_keys
    base_values = tail_values
    base_keys = base_keys + own_grad_keys
    base_values = base_values + own_grad_values
    key_total = key_acc + unpool_rows(base_keys)
    value_total = value_acc + unpool_rows(base_values)
    query_out = query_total.astype(jnp.bfloat16).reshape(token_rows, -1)
    key_out = key_total.astype(jnp.bfloat16).reshape(token_rows, -1)
    value_out = value_total.astype(jnp.bfloat16).reshape(token_rows, -1)
    return (
        lax.all_to_all(attended, "head", split_axis=0, concat_axis=1, tiled=True),
        lax.all_to_all(query_out, "head", split_axis=0, concat_axis=1, tiled=True),
        lax.all_to_all(key_out, "head", split_axis=0, concat_axis=1, tiled=True),
        lax.all_to_all(value_out, "head", split_axis=0, concat_axis=1, tiled=True),
    )


def solution(mesh):
    in_specs = (
        P(("seq", "head"), None),
        P(("seq", "head"), None),
        P(("seq", "head"), None),
        P(("seq", "head"), None),
    )
    out_specs = (
        P(("seq", "head"), None),
        P(("seq", "head"), None),
        P(("seq", "head"), None),
        P(("seq", "head"), None),
    )
    return jax.shard_map(local, mesh=mesh, in_specs=in_specs, out_specs=out_specs, check_vma=False)
```

profile of v0, /device:TPU:8, one launch (start us, length us, event | category | flops | bytes accessed | tf_op | source)
XLA Modules:
  0.0 1857.8 jit_solution(11937206118050483747)
XLA Ops:
  7.2 1.7 copy.2307
  8.8 5.7 all-to-all-start.1
  18.7 4.5 all-to-all-start
  24.6 1.8 all-to-all-done
  26.4 5.4 all-to-all-start.2
  35.5 4.9 all-to-all-start.4
  42.0 184.1 %all-gather = bf16[128,1,8,128]{3,2,1,0:T(8,128)(2,1)S(1)} all-gather(bf16[1,1,8,128]{3,2,1,0:T(8,128)(2,1)S(1)} %fusion.264), channel_id=2, replica_groups=mesh['seq'=128,'head'=2] {'seq'}, dimensions={0}, use_global_device_ids=true | all-gather | bytes 264192 | tf_op jit(solution)/shard_map/all_gather | solution.py:66
  226.7 175.9 %all-gather.1 = bf16[128,1,8,128]{3,2,1,0:T(8,128)(2,1)S(1)} all-gather(bf16[1,1,8,128]{3,2,1,0:T(8,128)(2,1)S(1)} %fusion.260), channel_id=3, replica_groups=mesh['seq'=128,'head'=2] {'seq'}, dimensions={0}, use_global_device_ids=true | all-gather | bytes 264192 | tf_op jit(solution)/shard_map/all_gather | solution.py:67
  404.3 0.9 copy.1701
  410.0 1.8 collective-permute-start.1
  417.4 1.0 copy.1653
  428.2 1.0 broadcast_select_fusion.13
  430.3 3.5 collective-permute-start.8
  434.9 1.0 copy.1659
  449.7 1.0 copy.1664
  450.7 0.9 broadcast_select_fusion.9
  452.2 3.6 collective-permute-start.9
  463.9 0.9 broadcast_select_fusion.7
  465.8 1.0 copy.1669
  467.4 2.1 collective-permute-start.10
  480.1 1.0 copy.1674
  481.2 0.9 broadcast_select_fusion.1
  482.6 3.2 collective-permute-start.11
  495.8 1.0 copy.1679
  498.4 1.4 fusion.281
  501.2 3.7 multiply_reduce_fusion.4
  505.7 1.4 reduce_sum.256
  507.8 1.3 reduce_sum.248
  509.8 1.3 reduce_sum.252
  513.4 0.9 fusion.18
  516.5 1.0 mul.1134
  517.5 1.1 mul.1135
  519.3 1.0 fusion.60
  533.6 0.9 fusion.53
  534.5 2.2 collective-permute-start.12
  545.4 0.8 copy-done.5
  546.5 0.8 copy-done.17
  549.0 0.8 all_to_all.120
  549.8 4.8 all-to-all-start.5
  554.9 0.8 all_to_all.113
  557.8 0.9 convert_multiply_fusion
  559.9 0.9 convert_multiply_fusion.1
  561.8 2.3 collective-permute-start.13
  566.2 1.0 collective-permute-done.13
  568.3 2.6 collective-permute-start.14
  571.0 1.7 collective-permute-done.20
  574.0 0.9 collective-permute-done.14
  576.1 2.7 collective-permute-start.15
  578.8 1.8 collective-permute-done.21
  581.2 3.0 collective-permute-start.22
  584.7 0.9 collective-permute-start.16
  585.6 1.5 collective-permute-done.22
  587.7 2.1 collective-permute-done.16
  590.3 1227.6 %all-reduce.5.cloned.1.call-done = (f32[128,8,128]{2,1,0:T(8,128)}, f32[128,8,128]{2,1,0:T(8,128)}) async-done(((f32[128,8,128]{2,1,0:T(8,128)}, f32[128,8,128]{2,1,0:T(8,128)}), (f32[128,8,128]{2,1,0:T(8,128)}, f32[128,8,128]{2,1,0:T(8,128)})) %all-reduce.5.cloned.1.call-update) | async-done | bytes 1048592
  1817.9 1.3 fusion.265
  1820.8 0.8 all_to_all.128
  1821.6 1.3 fusion.266
  1822.9 4.9 all-to-all-start.3
  1827.9 4.1 all-to-all-done.3
  1832.1 5.6 all-to-all-start.7
  1838.3 0.8 all_to_all.124
  1839.1 2.6 all-to-all-done.7
  1841.7 5.2 all-to-all-start.6
  1846.9 1.7 copy.1949
  (856 shorter events, 128.9 us)
Async XLA Ops:
  8.8 5.8 copy-start.39
  8.8 9.9 all-to-all-start.1
  18.7 7.7 all-to-all-start
  26.4 9.1 all-to-all-start.2
  34.8 374.6 %collective-permute-start = (bf16[64,8,128]{2,0,1:T(8,128)(2,1)S(1)}, bf16[64,8,128]{2,0,1:T(8,128)(2,1)S(1)}, u32[]{:S(2)}, u32[]{:S(2)}) collective-permute-start(bf16[64,8,128]{2,0,1:T(8,128)(2,1)S(1)} %bitcast.781), channel_id=1, source_target_pairs={{0,2},{2,0},{4,6},{6,4},{8,10},{10,8},{12,14},{14,12},{16,18},{18,... | collective-permute-start | bytes 393224 | tf_op jit(solution)/shard_map/ppermute | solution.py:18
  35.5 368.7 %all-to-all-start.4 = ((bf16[64,2,1024]{2,0,1:T(8,128)(2,1)}), bf16[64,2,1024]{2,0,1:T(8,128)(2,1)S(1)}, u32[]{:S(2)}, u32[]{:S(2)}) async-start(bf16[64,2,1024]{2,0,1:T(8,128)(2,1)} %bitcast.706), calls=%async_computation.4 | async-start | bytes 524288 | tf_op jit(solution)/shard_map/all_to_all | solution.py:36
  40.7 368.7 %collective-permute-start.6 = (bf16[64,8,128]{2,0,1:T(8,128)(2,1)S(1)}, bf16[64,8,128]{2,0,1:T(8,128)(2,1)S(1)}, u32[]{:S(2)}, u32[]{:S(2)}) collective-permute-start(bf16[64,8,128]{2,0,1:T(8,128)(2,1)S(1)} %bitcast.783), channel_id=1, source_target_pairs={{0,2},{2,0},{4,6},{6,4},{8,10},{10,8},{12,14},{14,12},{16,18},{18,... | collective-permute-start | bytes 393224 | tf_op jit(solution)/shard_map/ppermute | solution.py:18
  403.2 4.8 copy-start.66
  409.4 7.6 copy-start.14
  410.0 13.9 collective-permute-start.1
  412.0 5.0 copy-start.48
  416.0 12.2 collective-permute-start.7
  424.5 16.9 collective-permute-start.2
  428.2 6.3 copy-start.2
  430.3 19.1 %collective-permute-start.8 = (bf16[64,8,128]{2,0,1:T(8,128)(2,1)}, bf16[64,8,128]{2,0,1:T(8,128)(2,1)S(1)}, u32[]{:S(2)}, u32[]{:S(2)}) collective-permute-start(bf16[64,8,128]{2,0,1:T(8,128)(2,1)} %fusion.136), channel_id=1, source_target_pairs={{0,8},{8,0},{2,10},{10,2},{4,12},{12,4},{6,14},{14,6},{16,24},{24,... | collective-permute-start | bytes 393224 | tf_op jit(solution)/shard_map/ppermute | solution.py:18
  441.4 6.8 copy-start.6
  443.3 4.2 copy-start.99
  449.4 9.1 collective-permute-start.3
  452.1 3.7 copy-start.96
  452.2 6.6 copy-start.23
  452.2 13.2 collective-permute-start.9
  458.6 5.3 copy-start.10
  458.8 6.7 copy-start.27
  458.8 14.1 copy-start.50
  461.9 8.9 copy-start.101
  465.4 8.3 collective-permute-start.4
  467.4 6.3 copy-start.21
  467.4 12.0 collective-permute-start.10
  473.7 4.5 copy-start.12
  473.9 5.5 copy-start.57
  473.9 15.5 copy-start.52
  479.4 11.3 collective-permute-start.5
  482.5 3.3 copy-start.166
  482.6 12.5 collective-permute-start.11
  491.0 4.1 copy-start.93
  495.8 5.4 copy-start.32
  501.2 12.1 copy-start.44
  504.9 8.4 copy-start.42
  519.3 2.8 copy-start.177
  519.3 2.8 copy-start.178
  519.3 2.8 copy-start.179
  520.3 37.5 %collective-permute-start.18 = (bf16[64,8,128]{2,0,1:T(8,128)(2,1)}, bf16[64,8,128]{2,0,1:T(8,128)(2,1)}, u32[]{:S(2)}, u32[]{:S(2)}) collective-permute-start(bf16[64,8,128]{2,0,1:T(8,128)(2,1)} %fusion.60), channel_id=1, source_target_pairs={{0,64},{64,0},{2,66},{66,2},{4,68},{68,4},{6,70},{70,6},{8,72},{72... | collective-permute-start | bytes 393224 | tf_op jit(solution)/shard_map/ppermute | solution.py:18
  533.6 3.2 copy-start.65
  534.5 25.4 %collective-permute-start.12 = (bf16[64,8,128]{2,0,1:T(8,128)(2,1)}, bf16[64,8,128]{2,0,1:T(8,128)(2,1)}, u32[]{:S(2)}, u32[]{:S(2)}) collective-permute-start(bf16[64,8,128]{2,0,1:T(8,128)(2,1)} %fusion.53), channel_id=1, source_target_pairs={{0,64},{64,0},{2,66},{66,2},{4,68},{68,4},{6,70},{70,6},{8,72},{72... | collective-permute-start | bytes 393224 | tf_op jit(solution)/shard_map/ppermute | solution.py:18
  537.2 3.4 copy-start.37
  540.4 3.0 copy-start.171
  540.6 3.6 copy-start.121
  541.5 2.9 copy-start.35
  549.8 4.9 copy-start.45
  549.8 1273.1 %all-to-all-start.5 = ((bf16[2,64,1024]{2,1,0:T(8,128)(2,1)}), bf16[2,64,1024]{2,1,0:T(8,128)(2,1)}, u32[]{:S(2)}, u32[]{:S(2)}) async-start(bf16[2,64,1024]{2,1,0:T(8,128)(2,1)} %all_to_all.120), calls=%async_computation.5 | async-start | bytes 524288 | tf_op jit(solution)/shard_map/all_to_all | solution.py:234
  554.7 1263.3 %all-reduce.5.cloned.1.call-start = ((), (), s32[]{:S(2)}) async-start(), calls=%async_computation.8 | async-start | bytes 2097152
  559.8 5.1 collective-permute-start.19
  561.8 5.3 collective-permute-start.13
  566.1 6.6 collective-permute-start.20
  568.3 6.6 collective-permute-start.14
  573.9 6.7 collective-permute-start.21
  576.1 8.1 collective-permute-start.15
  581.2 5.9 collective-permute-start.22
  584.7 5.1 collective-permute-start.16
  587.6 1231.6 %collective-permute-start.23 = (bf16[64,8,128]{2,0,1:T(8,128)(2,1)S(1)}, bf16[64,8,128]{2,0,1:T(8,128)(2,1)S(1)}, u32[]{:S(2)}, u32[]{:S(2)}) collective-permute-start(bf16[64,8,128]{2,0,1:T(8,128)(2,1)S(1)} %fusion.46), channel_id=1, source_target_pairs={{0,2},{2,0},{4,6},{6,4},{8,10},{10,8},{12,14},{14,12},{16,18},{18,... | collective-permute-start | bytes 393224 | tf_op jit(solution)/shard_map/ppermute | solution.py:18
  590.2 1237.6 %collective-permute-start.17 = (bf16[64,8,128]{2,0,1:T(8,128)(2,1)S(1)}, bf16[64,8,128]{2,0,1:T(8,128)(2,1)S(1)}, u32[]{:S(2)}, u32[]{:S(2)}) collective-permute-start(bf16[64,8,128]{2,0,1:T(8,128)(2,1)S(1)} %fusion.48), channel_id=1, source_target_pairs={{0,2},{2,0},{4,6},{6,4},{8,10},{10,8},{12,14},{14,12},{16,18},{18,... | collective-permute-start | bytes 393224 | tf_op jit(solution)/shard_map/ppermute | solution.py:18
  1822.9 9.1 all-to-all-start.3
  1832.1 9.6 all-to-all-start.7
  1841.7 8.3 all-to-all-start.6
  (181 other events, 162.7 us)
Sparse Core Ops, SparseCore 0:
  558.1 1259.7 all-reduce.4
where the time goes:
time: 1870 us; the launch traced here: 1860 us
  waiting for transfers between devices  1250 us (67%)
  blocking collectives  360 us (19%)
  local copies, waits for them, and re-layouts  123 us (7%)
  starting transfers between devices  70.7 us (4%)
  other arithmetic  24.6 us (1%)
    unnamed x2, waiting for transfers between devices  1230 us
    all_gather x1, blocking collectives, local(): lax.all_gather(key_pool[level_count], 'seq', axis=0, tiled=True)  184 us
    all_gather x1, blocking collectives, local(): lax.all_gather(value_pool[level_count], 'seq', axis=0, tiled=True)  176 us
  transfers between devices with their start and end apart: 33, of which 13 were waited for; matrix products, arithmetic and copies ran while one was open for 6% of the time, Pallas kernels for 0%

commit v1 on v0

--- a/solution.py
+++ b/solution.py
@@ -6,6 +6,15 @@
 
 HEAD_DIM = 128
 ROOT_HALF = 0.7071067811865476
+weights_fill = lambda my_tile, axis_tag: jnp.concatenate(
+    lax.all_to_all(
+        jnp.stack([my_tile for _ in range(lax.axis_size(axis_tag))]),
+        axis_name=axis_tag,
+        split_axis=0,
+        concat_axis=0,
+    ),
+    axis=0,
+)
 
 
 def swapped(block, axis, distance):
@@ -63,7 +72,7 @@
             sib_keys, sib_values = swapped((own_keys, own_values), "seq", level_no - 1)
         else:
             whole_keys, whole_values = (
-                lax.all_gather(key_pool[level_count], "seq", axis=0, tiled=True),
+                weights_fill(key_pool[level_count], "seq"),
                 lax.all_gather(value_pool[level_count], "seq", axis=0, tiled=True),
             )
             sib_keys = lax.dynamic_slice_in_dim(whole_keys, sibling_start, half_rows, 0)

time: 1870 us -> 1730 us (0.925)
  blocking collectives: 360 us -> 194 us
    all_gather x1 -> x0, blocking collectives: 184 us -> none  [local(): lax.all_gather(key_pool[level_count], 'seq', axis=0, tiled=True)]
  transfers between devices with their start and end apart: 33 -> 34, of which waited for: 13 -> 12; matrix products, arithmetic and copies ran while one was open for 6% -> 7% of each run, Pallas kernels for 0% -> 0%
where the time goes in v1:
time: 1730 us; the launch traced here: 1720 us
  waiting for transfers between devices  1250 us (72%)
  blocking collectives  194 us (11%)
  local copies, waits for them, and re-layouts  123 us (7%)
  starting transfers between devices  82.5 us (5%)
  other arithmetic  25.4 us (1%)
  matrix products  19.8 us (1%)
    unnamed x2, waiting for transfers between devices  1230 us
    all_gather x1, blocking collectives, local(): lax.all_gather(value_pool[level_count], 'seq', axis=0, tiled=True)  194 us
  transfers between devices with their start and end apart: 34, of which 12 were waited for; matrix products, arithmetic and copies ran while one was open for 7% of the time, Pallas kernels for 0%

profile of v1, /device:TPU:8, one launch (start us, length us, event | category | flops | bytes accessed | tf_op | source)
XLA Modules:
  0.0 1716.3 jit_solution(79401301146423357)
XLA Ops:
  7.2 1.7 copy.2301
  8.8 5.7 all-to-all-start.1
  18.7 4.5 all-to-all-start.3
  25.2 1.1 all-to-all-done.3
  26.4 5.4 all-to-all-start
  32.8 2.1 all-to-all-done
  35.0 5.4 all-to-all-start.5
  43.6 194.4 %all-gather = bf16[128,1,8,128]{3,2,1,0:T(8,128)(2,1)} all-gather(bf16[1,1,8,128]{3,2,1,0:T(8,128)(2,1)S(1)} %fusion.260), channel_id=2, replica_groups=mesh['seq'=128,'head'=2] {'seq'}, dimensions={0}, use_global_device_ids=true | all-gather | bytes 264192 | tf_op jit(solution)/shard_map/all_gather | solution.py:76
  241.0 7.3 all-to-all-start.2
  254.0 1.0 collective-permute-start.1
  259.2 1.1 collective-permute-start.7
  261.4 1.0 copy.1647
  268.5 3.0 collective-permute-start.2
  274.7 1.0 broadcast_select_fusion.13
  276.9 1.1 collective-permute-start.8
  278.9 1.0 copy.1653
  293.5 2.5 collective-permute-start.3
  297.7 1.0 copy.1658
  299.3 1.1 collective-permute-start.9
  305.8 1.1 fusion.315
  312.1 1.0 broadcast_select_fusion.7
  313.6 1.1 collective-permute-start.4
  315.0 1.0 copy.1663
  317.2 1.0 collective-permute-start.10
  327.6 2.2 collective-permute-start.5
  329.8 1.1 convolution_bitcast_fusion.17
  331.0 1.0 copy.1668
  332.0 1.0 broadcast_select_fusion.1
  333.6 1.0 collective-permute-start.11
  344.0 1.0 copy.1673
  346.5 1.4 fusion.282
  349.3 3.7 multiply_reduce_fusion.4
  353.8 1.4 reduce_sum.256
  355.9 1.3 reduce_sum.248
  357.9 1.4 reduce_sum.252
  361.6 0.9 fusion.18
  364.6 1.0 mul.1128
  365.6 1.1 mul.1129
  367.4 1.0 fusion.60
  368.4 2.1 collective-permute-start.18
  387.6 1.1 fusion.82
  392.6 1.1 fusion.71
  398.3 6.9 all-to-all-start.6
  408.3 0.9 convert_multiply_fusion
  410.3 1.5 collective-permute-start.19
  414.7 1.6 collective-permute-done.19
  417.5 2.2 collective-permute-start.20
  420.9 1.9 collective-permute-start.14
  422.8 1.3 collective-permute-done.20
  425.3 3.1 collective-permute-start.21
  429.6 2.1 collective-permute-start.15
  431.7 1.3 collective-permute-done.21
  433.6 1.0 collective-permute-start.22
  434.6 2.7 collective-permute-done.15
  439.2 3.7 collective-permute-done.16
  443.4 1232.9 %all-reduce.5.cloned.1.call-done = (f32[128,8,128]{2,1,0:T(8,128)}, f32[128,8,128]{2,1,0:T(8,128)}) async-done(((f32[128,8,128]{2,1,0:T(8,128)}, f32[128,8,128]{2,1,0:T(8,128)}), (f32[128,8,128]{2,1,0:T(8,128)}, f32[128,8,128]{2,1,0:T(8,128)})) %all-reduce.5.cloned.1.call-update) | async-done | bytes 1048592
  1676.3 1.3 fusion.265
  1680.0 1.3 fusion.266
  1681.4 4.9 all-to-all-start.4
  1686.4 4.1 all-to-all-done.4
  1690.5 5.6 all-to-all-start.8
  1697.6 2.6 all-to-all-done.8
  1700.1 5.2 all-to-all-start.7
  1705.3 1.7 copy.1943
  (855 shorter events, 137.3 us)
Async XLA Ops:
  8.8 5.8 copy-start.37
  8.8 9.9 all-to-all-start.1
  18.7 7.7 all-to-all-start.3
  26.4 8.6 all-to-all-start
  32.1 220.6 %collective-permute-start.6 = (bf16[64,8,128]{2,0,1:T(8,128)(2,1)S(1)}, bf16[64,8,128]{2,0,1:T(8,128)(2,1)S(1)}, u32[]{:S(2)}, u32[]{:S(2)}) collective-permute-start(bf16[64,8,128]{2,0,1:T(8,128)(2,1)S(1)} %bitcast.782), channel_id=1, source_target_pairs={{0,2},{2,0},{4,6},{6,4},{8,10},{10,8},{12,14},{14,12},{16,18},{18,... | collective-permute-start | bytes 393224 | tf_op jit(solution)/shard_map/ppermute | solution.py:27
  35.0 8.6 all-to-all-start.5
  40.7 212.0 %collective-permute-start = (bf16[64,8,128]{2,0,1:T(8,128)(2,1)S(1)}, bf16[64,8,128]{2,0,1:T(8,128)(2,1)S(1)}, u32[]{:S(2)}, u32[]{:S(2)}) collective-permute-start(bf16[64,8,128]{2,0,1:T(8,128)(2,1)S(1)} %bitcast.784), channel_id=1, source_target_pairs={{0,2},{2,0},{4,6},{6,4},{8,10},{10,8},{12,14},{14,12},{16,18},{18,... | collective-permute-start | bytes 393224 | tf_op jit(solution)/shard_map/ppermute | solution.py:27
  43.5 196.6 %copy-start.53 = (f32[128,8]{0,1:T(8,128)}, f32[128,8]{0,1:T(8,128)S(1)}, u32[]{:S(2)}) copy-start(f32[128,8]{0,1:T(8,128)S(1)} %get-tuple-element.128) | copy-start | bytes 12292
  241.0 62.1 %all-to-all-start.2 = ((bf16[128,1,8,128]{3,2,1,0:T(8,128)(2,1)}), bf16[128,1,8,128]{3,2,1,0:T(8,128)(2,1)}, u32[]{:S(2)}, u32[]{:S(2)}) async-start(bf16[128,1,8,128]{3,2,1,0:T(8,128)(2,1)} %stack.5), calls=%async_computation.2 | async-start | bytes 524288 | tf_op jit(solution)/shard_map/all_to_all | solution.py:10
  249.2 2.8 copy-start.19
  252.7 8.3 copy-start.12
  252.7 2.4 copy-start.14
  254.0 13.9 collective-permute-start.1
  255.3 5.7 copy-start.46
  259.2 15.5 collective-permute-start.7
  268.0 3.6 copy-start.4
  268.5 16.9 collective-permute-start.2
  274.7 3.9 copy-start.2
  276.9 19.2 %collective-permute-start.8 = (bf16[64,8,128]{2,0,1:T(8,128)(2,1)}, bf16[64,8,128]{2,0,1:T(8,128)(2,1)S(1)}, u32[]{:S(2)}, u32[]{:S(2)}) collective-permute-start(bf16[64,8,128]{2,0,1:T(8,128)(2,1)} %fusion.136), channel_id=1, source_target_pairs={{0,8},{8,0},{2,10},{10,2},{4,12},{12,4},{6,14},{14,6},{16,24},{24,... | collective-permute-start | bytes 393224 | tf_op jit(solution)/shard_map/ppermute | solution.py:27
  285.5 6.8 copy-start.6
  287.4 4.2 copy-start.96
  293.5 12.3 collective-permute-start.3
  299.3 15.5 collective-permute-start.9
  307.0 14.7 copy-start.48
  310.1 9.5 copy-start.98
  313.6 8.8 collective-permute-start.4
  317.2 12.6 collective-permute-start.10
  322.4 4.6 copy-start.10
  322.7 15.5 copy-start.50
  327.5 2.3 copy-start.56
  327.6 11.3 collective-permute-start.5
  333.6 9.7 collective-permute-start.11
  339.2 4.1 copy-start.90
  344.0 5.3 copy-start.28
  349.3 12.1 copy-start.42
  353.0 8.4 copy-start.40
  367.4 3.1 copy-start.45
  367.4 4.2 copy-start.174
  367.4 4.2 copy-start.175
  367.4 4.2 copy-start.176
  368.4 39.9 %collective-permute-start.18 = (bf16[64,8,128]{2,0,1:T(8,128)(2,1)}, bf16[64,8,128]{2,0,1:T(8,128)(2,1)}, u32[]{:S(2)}, u32[]{:S(2)}) collective-permute-start(bf16[64,8,128]{2,0,1:T(8,128)(2,1)} %fusion.60), channel_id=1, source_target_pairs={{0,64},{64,0},{2,66},{66,2},{4,68},{68,4},{6,70},{70,6},{8,72},{72... | collective-permute-start | bytes 393224 | tf_op jit(solution)/shard_map/ppermute | solution.py:27
  377.8 2.4 copy-start.70
  384.0 27.9 %collective-permute-start.12 = (bf16[64,8,128]{2,0,1:T(8,128)(2,1)}, bf16[64,8,128]{2,0,1:T(8,128)(2,1)}, u32[]{:S(2)}, u32[]{:S(2)}) collective-permute-start(bf16[64,8,128]{2,0,1:T(8,128)(2,1)} %fusion.53), channel_id=1, source_target_pairs={{0,64},{64,0},{2,66},{66,2},{4,68},{68,4},{6,70},{70,6},{8,72},{72... | collective-permute-start | bytes 393224 | tf_op jit(solution)/shard_map/ppermute | solution.py:27
  385.3 3.6 copy-start.35
  385.7 3.0 copy-start.94
  388.7 3.0 copy-start.168
  388.9 3.6 copy-start.118
  389.8 3.8 copy-start.33
  398.3 6.9 copy-start.43
  398.3 1283.0 %all-to-all-start.6 = ((bf16[2,64,1024]{2,1,0:T(8,128)(2,1)}), bf16[2,64,1024]{2,1,0:T(8,128)(2,1)}, u32[]{:S(2)}, u32[]{:S(2)}) async-start(bf16[2,64,1024]{2,1,0:T(8,128)(2,1)} %all_to_all.124), calls=%async_computation.6 | async-start | bytes 524288 | tf_op jit(solution)/shard_map/all_to_all | solution.py:243
  405.2 1271.1 %all-reduce.5.cloned.1.call-start = ((), (), s32[]{:S(2)}) async-start(), calls=%async_computation.9 | async-start | bytes 2097152
  410.3 5.9 collective-permute-start.19
  413.8 6.0 collective-permute-start.13
  417.5 6.6 collective-permute-start.20
  420.9 7.5 collective-permute-start.14
  425.3 7.7 collective-permute-start.21
  429.6 7.8 collective-permute-start.15
  433.6 5.1 collective-permute-start.22
  437.9 5.1 collective-permute-start.16
  439.1 1238.6 %collective-permute-start.23 = (bf16[64,8,128]{2,0,1:T(8,128)(2,1)S(1)}, bf16[64,8,128]{2,0,1:T(8,128)(2,1)S(1)}, u32[]{:S(2)}, u32[]{:S(2)}) collective-permute-start(bf16[64,8,128]{2,0,1:T(8,128)(2,1)S(1)} %fusion.46), channel_id=1, source_target_pairs={{0,2},{2,0},{4,6},{6,4},{8,10},{10,8},{12,14},{14,12},{16,18},{18,... | collective-permute-start | bytes 393224 | tf_op jit(solution)/shard_map/ppermute | solution.py:27
  443.3 1242.9 %collective-permute-start.17 = (bf16[64,8,128]{2,0,1:T(8,128)(2,1)S(1)}, bf16[64,8,128]{2,0,1:T(8,128)(2,1)S(1)}, u32[]{:S(2)}, u32[]{:S(2)}) collective-permute-start(bf16[64,8,128]{2,0,1:T(8,128)(2,1)S(1)} %fusion.48), channel_id=1, source_target_pairs={{0,2},{2,0},{4,6},{6,4},{8,10},{10,8},{12,14},{14,12},{16,18},{18,... | collective-permute-start | bytes 393224 | tf_op jit(solution)/shard_map/ppermute | solution.py:27
  1681.4 9.1 all-to-all-start.4
  1690.5 9.6 all-to-all-start.8
  1700.1 8.3 all-to-all-start.7
  (180 other events, 160.6 us)
Sparse Core Ops, SparseCore 0:
  408.6 1267.6 all-reduce.4
